TPU v7x, 128 devices: a whole 4x4x4 slice. The times are simulated.
128 devices in a mesh: dp: 2 (over x_lo), space: 64 (over z, y, x_hi, core).
Axes of the slice: x: 4 (x_hi: 2, x_lo: 2; x = x_hi * 2 + x_lo), y: 4, z: 4, core: 2. Of those that a mesh axis runs over, the one named last changes fastest.
Arguments:
- stash: bfloat16 [64, 64, 4, 2160], P('space', None, 'dp'), may hold values from -5 to 5
- piece_map: int32 [64, 64], P(None, 'space'), may hold values from 0 to 63, as said below
- gain_one: float32 [768], replicated, may hold values from 0.5 to 1.5
- spec_one: float32 [2, 8, 96, 96], replicated, may hold values from -0.4375 to 0.4375
- bias_one: float32 [2, 768], replicated, may hold values from -3 to 3
- spec_two: float32 [2, 8, 96, 96], replicated, may hold values from -0.4375 to 0.4375
- bias_two: float32 [2, 768], replicated, may hold values from -0.6 to 0.6
- gain_two: float32 [768], replicated, may hold values from 0.5 to 1.5
- fc_one: bfloat16 [768, 3072], replicated, may hold values from -0.21875 to 0.21875
- bias_fc: float32 [3072], replicated, may hold values from -3 to 3
- fc_two: bfloat16 [3072, 768], replicated, may hold values from -0.109375 to 0.109375
- cotangent: bfloat16 [4, 64, 180, 768], P('dp', 'space'), may hold values from -6 to 6
Outputs:
- grad_input: float32 [4, 64, 180, 768], P('dp', 'space')
- grad_fc_one: float32 [768, 3072], P(None, ('dp', 'space'))
- grad_fc_two: float32 [3072, 768], P(('dp', 'space'))
- grad_bias_fc: float32 [3072], replicated
- grad_bias_out: float32 [768], replicated
- grad_gain_one: float32 [768], replicated
- grad_gain_two: float32 [768], replicated
- grad_spec_one: float32 [2, 8, 96, 96], replicated
- grad_bias_one: float32 [2, 768], replicated
- grad_spec_two: float32 [2, 8, 96, 96], replicated
- grad_bias_two: float32 [2, 768], replicated
Inputs may be any that keep to these rules, and one draw needn't show every extreme that they name: `piece_map`: each column holds every number from 0 to 63 once.
All inputs are finite; a program needn't handle non-finite values.
Results may differ from a plain program's by a relative error of at most 0.0046.
Values may be sent and summed in bfloat16 or wider, within the bound.
No kernel may reach another device: no remote copies, remote signals or barrier semaphores. Data moves between devices by JAX's collectives and lax.ppermute only.
A program may use at most 128 MiB of HBM per device.

v0:
```python
import math
import jax
import jax.numpy as jnp
from jax import lax
from jax.sharding import PartitionSpec as P

KW = 64
epsilon = 1e-05
highest = lax.Precision.HIGHEST


def in_one_piece(arrays, axis, split_dim, concat_dim, along):
    both = jnp.concatenate(arrays, axis=along)
    result, at, finished = (
        lax.all_to_all(both, axis, split_axis=split_dim, concat_axis=concat_dim, tiled=True),
        0,
        [],
    )
    for a in arrays:
        finished.append(lax.slice_in_dim(result, at, at + a.shape[along], axis=along))
        at += a.shape[along]
    return tuple(finished)


def side_by_side(arrays, axis, dim, along):
    widths = [a.shape[along] for a in arrays]
    both = jnp.concatenate(arrays, axis=along)
    result = lax.psum_scatter(both, axis, scatter_dimension=dim, tiled=True)
    return tuple(jnp.split(result, [sum(widths[:k]) for k in range(1, len(widths))], axis=along))


def layer_norm(values, gain_vector):
    centred = values - jnp.mean(values, axis=-1, keepdims=True)
    spread = jnp.mean(centred * centred, axis=-1, keepdims=True)
    return centred * lax.rsqrt(spread + epsilon) * gain_vector


def smooth_gate(values):
    return jax.nn.gelu(values, approximate=True)


def block_mix(real_part, imag_part, weights, biases):
    blocks = weights.shape[1]
    width_block = weights.shape[2]
    leading = real_part.shape[:-1]
    real_blocks = real_part.reshape(leading + (blocks, width_block))
    imag_blocks = imag_part.reshape(leading + (blocks, width_block))
    bias_real = biases[0].reshape(blocks, width_block)
    bias_imag = biases[1].reshape(blocks, width_block)
    new_real = (
        jnp.einsum("...ni,nio->...no", real_blocks, weights[0], precision=highest)
        - jnp.einsum("...ni,nio->...no", imag_blocks, weights[1], precision=highest)
        + bias_real
    )
    new_imag = (
        jnp.einsum("...ni,nio->...no", real_blocks, weights[1], precision=highest)
        + jnp.einsum("...ni,nio->...no", imag_blocks, weights[0], precision=highest)
        + bias_imag
    )
    return (
        new_real.reshape(leading + (blocks * width_block,)),
        new_imag.reshape(leading + (blocks * width_block,)),
    )


def spectral_mlp(spec_real, spec_imag, spec_one, bias_one, spec_two, bias_two):
    inner_real, inner_imag = block_mix(spec_real, spec_imag, spec_one, bias_one)
    return block_mix(smooth_gate(inner_real), smooth_gate(inner_imag), spec_two, bias_two)


def wave_tables(length, total_modes):
    positions = jnp.arange(length, dtype=jnp.int32)
    frequency = jnp.arange(total_modes, dtype=jnp.int32)
    phases = positions[:, None] * frequency[None, :] % length
    angles = phases.astype(jnp.float32) * (2.0 * math.pi / length)
    factor = 1.0 / math.sqrt(length)
    return (jnp.cos(angles) * factor, jnp.sin(angles) * factor)


def meridian_apply(table, field):
    return jnp.einsum("hk,bhmd->bkmd", table, field, precision=highest)


def meridian_forward(real_part, imag_part, merid_cos, merid_sin):
    new_real = meridian_apply(merid_cos, real_part) + meridian_apply(merid_sin, imag_part)
    new_imag = meridian_apply(merid_cos, imag_part) - meridian_apply(merid_sin, real_part)
    return (new_real, new_imag)


def meridian_inverse(real_part, imag_part, merid_cos, merid_sin):
    new_real = meridian_apply(merid_cos, real_part) - meridian_apply(merid_sin, imag_part)
    new_imag = meridian_apply(merid_cos, imag_part) + meridian_apply(merid_sin, real_part)
    return (new_real, new_imag)


def zonal_project(field, table):
    return jnp.einsum("brwd,wk->brkd", field, table, precision=highest)


def zonal_expand(field, table):
    return jnp.einsum("brkd,wk->brwd", field, table, precision=highest)


def local(
    stash,
    piece_map,
    gain_one,
    spec_one,
    bias_one,
    spec_two,
    bias_two,
    gain_two,
    fc_one,
    bias_fc,
    fc_two,
    cotangent,
):
    samples, lat_rows, lon_cells, model_width = cotangent.shape
    space_ranks = lax.axis_size("space")
    lat_total = lat_rows * space_ranks
    tokens = samples * lat_rows * lon_cells
    arrived = lax.all_to_all(stash, "space", split_axis=1, concat_axis=0, tiled=True)
    ordering = jnp.argsort(piece_map[:, 0])
    placed = jnp.take(arrived[:, 0], ordering, axis=0)
    inputs = jnp.transpose(placed, (1, 0, 2)).reshape(samples, lat_rows, lon_cells, model_width)
    base_field = inputs.astype(jnp.float32)
    zonal_cos, zonal_sin = wave_tables(lon_cells, KW)
    doubling = jnp.where(jnp.arange(KW) == 0, 1.0, 2.0).astype(jnp.float32)
    back_cos = zonal_cos * doubling
    back_sin = zonal_sin * doubling
    merid_cos, merid_sin = wave_tables(lat_total, lat_total)
    normed, pull_one = jax.vjp(layer_norm, base_field, gain_one)
    zonal_real = zonal_project(normed, zonal_cos)
    zonal_imag = -zonal_project(normed, zonal_sin)
    modes_real, modes_imag = in_one_piece((zonal_real, zonal_imag), "space", 2, 1, 0)
    spec_real, spec_imag = meridian_forward(modes_real, modes_imag, merid_cos, merid_sin)
    mixed_spec, pull_mix = jax.vjp(
        spectral_mlp, spec_real, spec_imag, spec_one, bias_one, spec_two, bias_two
    )
    back_real, back_imag = meridian_inverse(mixed_spec[0], mixed_spec[1], merid_cos, merid_sin)
    rows_real, rows_imag = in_one_piece((back_real, back_imag), "space", 1, 2, 0)
    spatial = zonal_expand(rows_real, back_cos) - zonal_expand(rows_imag, back_sin)
    mixed_field = base_field + normed + spatial
    normed_two, pull_two = jax.vjp(layer_norm, mixed_field, gain_two)
    normed_flat = normed_two.astype(jnp.bfloat16).reshape(tokens, model_width)
    hidden_pre = jnp.dot(normed_flat, fc_one, preferred_element_type=jnp.float32) + bias_fc
    active, pull_gate = jax.vjp(smooth_gate, hidden_pre)
    active_flat = active.astype(jnp.bfloat16)
    upstream = cotangent.reshape(tokens, model_width)
    grad_active = jnp.einsum("td,fd->tf", upstream, fc_two, preferred_element_type=jnp.float32)
    grad_hidden = pull_gate(grad_active)[0]
    grad_hidden_flat = grad_hidden.astype(jnp.bfloat16)
    grad_normed_two = jnp.einsum(
        "tf,df->td", grad_hidden_flat, fc_one, preferred_element_type=jnp.float32
    )
    term_one = jnp.einsum(
        "td,tf->df", normed_flat, grad_hidden_flat, preferred_element_type=jnp.float32
    )
    term_two = jnp.einsum("td,tf->df", upstream, active_flat, preferred_element_type=jnp.float32)
    grad_mixed_norm, grad_gain_two = pull_two(grad_normed_two.reshape(mixed_field.shape))
    grad_mixed = cotangent.astype(jnp.float32) + grad_mixed_norm
    grad_back_real = zonal_project(grad_mixed, back_cos)
    grad_back_imag = -zonal_project(grad_mixed, back_sin)
    grad_modes_real, grad_modes_imag = in_one_piece(
        (grad_back_real, grad_back_imag), "space", 2, 1, 0
    )
    grad_out_real, grad_out_imag = meridian_forward(
        grad_modes_real, grad_modes_imag, merid_cos, merid_sin
    )
    pulled = pull_mix((grad_out_real, grad_out_imag))
    grad_merid_real, grad_merid_imag = meridian_inverse(pulled[0], pulled[1], merid_cos, merid_sin)
    grad_rows_real, grad_rows_imag = in_one_piece(
        (grad_merid_real, grad_merid_imag), "space", 1, 2, 0
    )
    grad_normed = (
        grad_mixed
        + zonal_expand(grad_rows_real, zonal_cos)
        - zonal_expand(grad_rows_imag, zonal_sin)
    )
    grad_base, grad_gain_one = pull_one(grad_normed)
    grad_input = grad_mixed + grad_base
    bias_sum = jnp.sum(grad_hidden, axis=0)
    out_sum = jnp.sum(cotangent, axis=(0, 1, 2), dtype=jnp.float32)
    totals = lax.psum(
        (
            grad_gain_one,
            grad_gain_two,
            pulled[2],
            pulled[3],
            pulled[4],
            pulled[5],
            bias_sum,
            out_sum,
        ),
        ("dp", "space"),
    )
    paired = side_by_side((term_one, term_two), "dp", 1, 0)
    summed = side_by_side((paired[0], paired[1]), "space", 1, 0)
    grad_scale = 1.0 / math.sqrt(samples * lax.axis_size("dp") * lat_total * lon_cells)
    return (
        grad_input,
        summed[0] * grad_scale,
        (summed[1] * grad_scale).T,
        totals[6] * grad_scale,
        totals[7] * grad_scale,
        totals[0] * grad_scale,
        totals[1] * grad_scale,
        totals[2] * grad_scale,
        totals[3] * grad_scale,
        totals[4] * grad_scale,
        totals[5] * grad_scale,
    )


def solution(mesh):
    placed = (
        P("space", None, "dp", None),
        P(None, "space"),
        P(),
        P(),
        P(),
        P(),
        P(),
        P(),
        P(),
        P(),
        P(),
        P("dp", "space", None, None),
    )
    return jax.shard_map(
        local,
        mesh=mesh,
        in_specs=placed,
        out_specs=(
            P("dp", "space", None, None),
            P(None, ("dp", "space")),
            P(("dp", "space"), None),
            P(),
            P(),
            P(),
            P(),
            P(),
            P(),
            P(),
            P(),
        ),
        check_vma=False,
    )
```

profile of v0, /device:TPU:1, one launch (start us, length us, event | category | flops | bytes accessed | tf_op | source)
XLA Modules:
  0.0 582.4 jit_solution(12047435370016026344)
XLA Ops:
  8.0 12.5 %all-to-all-start = ((bf16[1,64,2,2160]{3,2,0,1:T(2,128)(2,1)}), bf16[1,64,2,2160]{3,2,0,1:T(2,128)(2,1)S(1)}, u32[]{:S(2)}, u32[]{:S(2)}) async-start(bf16[1,64,2,2160]{3,2,0,1:T(2,128)(2,1)} %bitcast.618), calls=%async_computation | async-start | bytes 1114112 | tf_op jit(solution)/shard_map/all_to_all | solution.py:122
  20.5 2.7 sort.17
  23.2 11.9 %all-to-all-done = bf16[1,64,2,2160]{3,2,0,1:T(2,128)(2,1)S(1)} async-done(((bf16[1,64,2,2160]{3,2,0,1:T(2,128)(2,1)}), bf16[1,64,2,2160]{3,2,0,1:T(2,128)(2,1)S(1)}, u32[]{:S(2)}, u32[]{:S(2)}) %all-to-all-start) | async-done | bytes 552992 | tf_op jit(solution)/shard_map/all_to_all | solution.py:122
  35.1 1.7 gather_fusion
  44.4 4.9 all-to-all-start.1
  49.6 16.6 %all-to-all-done.1 = f32[4,1,64,768]{3,0,1,2:T(4,128)S(1)} async-done(((f32[4,1,64,768]{3,0,1,2:T(4,128)}), f32[4,1,64,768]{3,0,1,2:T(4,128)S(1)}, u32[]{:S(2)}, u32[]{:S(2)}) %all-to-all-start.1) | async-done | bytes 786464 | tf_op jit(solution)/shard_map/all_to_all | solution.py:15
  74.4 1.9 convolution_subtract_fusion.2
  84.0 1.8 fusion.19
  89.9 4.7 all-to-all-start.2
  94.9 6.5 %fusion.414 = f32[360,3072]{1,0:T(8,128)} fusion(bf16[360,768]{1,0:T(8,128)(2,1)S(1)} %reshape.661, bf16[3072,768]{1,0:T(8,128)(2,1)} %param.22), kind=kOutput, calls=%fused_computation.519 | convolution fusion | flops 1698693120 | bytes 9695232 | tf_op jit(solution)/shard_map/td,fd->tf/dot_general | solution.py:150
  101.4 10.4 %all-to-all-done.2 = f32[4,64,1,768]{3,0,2,1:T(4,128)S(1)} async-done(((f32[4,64,1,768]{3,0,2,1:T(4,128)}), f32[4,64,1,768]{3,0,2,1:T(4,128)S(1)}, u32[]{:S(2)}, u32[]{:S(2)}) %all-to-all-start.2) | async-done | bytes 786464 | tf_op jit(solution)/shard_map/all_to_all | solution.py:15
  116.4 8.3 %fusion.404 = (f32[3072]{0:T(1024)S(1)}, bf16[360,3072]{1,0:T(8,128)(2,1)S(1)}, f32[360,3072]{1,0:T(8,128)S(1)}) fusion(f32[360,3072]{1,0:T(8,128)} %fusion.414, f32[3072]{0:T(1024)S(1)} %copy-done.30, bf16[360,768]{1,0:T(8,128)(2,1)S(1)} %reshape.672, bf16[768,3072]{1,0:T(8,128)(2,1)} %param.20), kind=kOutput, calls=%fused_computation.510 | convolution fusion | flops 1723020288 | bytes 16355328 | tf_op jit(solution)/shard_map/dot_general | solution.py:146
  124.8 2.7 fusion.32
  127.4 2.8 convolution_bitcast_fusion
  130.3 7.0 %pad_maximum_fusion = f32[1536,3072]{1,0:T(8,128)} fusion(f32[768,3072]{1,0:T(8,128)S(1)} %convolution_bitcast_fusion, f32[768,3072]{1,0:T(8,128)S(1)} %fusion.32), kind=kLoop, calls=%fused_computation.1 | loop fusion | flops 4718592 | bytes 37748736 | tf_op jit(solution)/shard_map/concatenate | solution.py:27
  137.8 6.0 %fusion.34 = f32[360,768]{1,0:T(8,128)} fusion(bf16[768,3072]{1,0:T(8,128)(2,1)} %param.20, bf16[360,3072]{1,0:T(8,128)(2,1)} %copy-done.16), kind=kOutput, calls=%fused_computation.87 | convolution fusion | flops 1698693120 | bytes 8036352 | tf_op jit(solution)/shard_map/tf,df->td/dot_general | solution.py:153
  147.2 1.7 convert_reduce_fusion
  151.6 30.1 %all_to_all.20 = f32[4,1,64,768]{3,0,1,2:T(4,128)S(1)} all-to-all(f32[4,1,64,768]{3,0,1,2:T(4,128)S(1)} %copy.78), channel_id=1, replica_groups=mesh['dp'=2,'space'=64] {'space'}, dimensions={2} | all-to-all | bytes 1572864 | tf_op jit(solution)/shard_map/all_to_all | solution.py:15
  187.6 2.2 convolution_bitcast_fusion.7
  196.6 2.0 fusion.70
  205.8 149.3 %reduce-scatter.5.cloned.1.call-done = f32[1536,1536]{1,0:T(8,128)} async-done(((f32[1536,3072]{1,0:T(8,128)}), f32[1536,1536]{1,0:T(8,128)}) %reduce-scatter.5.cloned.1.call-update) | async-done | bytes 9437200 | tf_op jit(solution)/shard_map/reduce_scatter | solution.py:28
  355.0 9.7 %copy.108 = f32[1536,1536]{0,1:T(8,128)} copy(f32[1536,1536]{1,0:T(8,128)} %reduce-scatter.5.cloned.1.call-done) | data formatting | bytes 18874368
  364.7 1.9 fusion.140
  368.6 2.0 reshape.686
  370.6 1.9 fusion.146
  379.7 12.2 %all-to-all-start.4 = ((f32[4,64,1,768]{3,0,2,1:T(4,128)}), f32[4,64,1,768]{3,0,2,1:T(4,128)S(1)}, u32[]{:S(2)}, u32[]{:S(2)}) async-start(f32[4,64,1,768]{3,0,2,1:T(4,128)} %copy.86), calls=%async_computation.4 | async-start | bytes 1572864 | tf_op jit(solution)/shard_map/all_to_all | solution.py:15
  392.0 1.6 fusion.48
  393.8 101.4 %all-reduce.16.cloned.1.call-done = (f32[2,8,96,96]{3,2,1,0:T(8,128)}, f32[2,8,96,96]{3,2,1,0:T(8,128)}) async-done(((f32[2,8,96,96]{3,2,1,0:T(8,128)}, f32[2,8,96,96]{3,2,1,0:T(8,128)}), (f32[2,8,96,96]{3,2,1,0:T(8,128)}, f32[2,8,96,96]{3,2,1,0:T(8,128)})) %all-reduce.16.cloned.1.call-update) | async-done | bytes 1179664 | tf_op jit(solution)/shard_map/psum | solution.py:184
  495.1 2.7 broadcast_multiply_fusion
  499.5 1.7 multiply_reduce_fusion.2
  502.2 2.1 copy.93
  504.3 64.9 %all-reduce.12 = (f32[3072]{0:T(1024)S(1)}, f32[768]{0:T(1024)S(1)}, f32[768]{0:T(1024)S(1)}, f32[768]{0:T(1024)S(1)}, f32[2,768]{1,0:T(2,128)S(1)}, /*index=5*/f32[2,768]{1,0:T(2,128)S(1)}) all-reduce(f32[3072]{0:T(1024)S(1)} %get-tuple-element.62, ...), channel_id=1, replica_groups=mesh['dp'=2,'space'=64] {'dp','space'}, use_global_device_ids=true, to_apply=%region_12.13 | all-reduce | flops 8448 | bytes 67584 | tf_op jit(solution)/shard_map/psum | solution.py:184
  (189 shorter events, 76.2 us)
Async XLA Ops:
  8.0 27.1 %all-to-all-start = ((bf16[1,64,2,2160]{3,2,0,1:T(2,128)(2,1)}), bf16[1,64,2,2160]{3,2,0,1:T(2,128)(2,1)S(1)}, u32[]{:S(2)}, u32[]{:S(2)}) async-start(bf16[1,64,2,2160]{3,2,0,1:T(2,128)(2,1)} %bitcast.618), calls=%async_computation | async-start | bytes 1114112 | tf_op jit(solution)/shard_map/all_to_all | solution.py:122
  44.4 4.9 copy-start.28
  44.4 5.0 copy-start.29
  44.4 21.8 %all-to-all-start.1 = ((f32[4,1,64,768]{3,0,1,2:T(4,128)}), f32[4,1,64,768]{3,0,1,2:T(4,128)S(1)}, u32[]{:S(2)}, u32[]{:S(2)}) async-start(f32[4,1,64,768]{3,0,1,2:T(4,128)} %copy.66), calls=%async_computation.1 | async-start | bytes 1572864 | tf_op jit(solution)/shard_map/all_to_all | solution.py:15
  68.5 1.1 copy-start.5
  69.7 2.1 copy-start.1
  69.7 2.1 copy-start.21
  74.4 4.4 copy-start.3
  74.4 1.9 copy-start.13
  79.4 4.5 copy-start.8
  80.3 3.7 copy-start.14
  85.8 1.2 copy-start.22
  89.9 4.7 copy-start.17
  89.9 21.8 %all-to-all-start.2 = ((f32[4,64,1,768]{3,0,2,1:T(4,128)}), f32[4,64,1,768]{3,0,2,1:T(4,128)S(1)}, u32[]{:S(2)}, u32[]{:S(2)}) async-start(f32[4,64,1,768]{3,0,2,1:T(4,128)} %copy.75), calls=%async_computation.2 | async-start | bytes 1572864 | tf_op jit(solution)/shard_map/all_to_all | solution.py:15
  94.6 260.4 %reduce-scatter.5.cloned.1.call-start = ((), (), s32[]{:S(2)}) async-start(), calls=%async_computation.7 | async-start | bytes 28311552 | tf_op jit(solution)/shard_map/reduce_scatter | solution.py:28
  94.9 6.5 %copy-start.23 = (bf16[360,768]{1,0:T(8,128)(2,1)}, bf16[360,768]{1,0:T(8,128)(2,1)S(1)}, u32[]{:S(2)}) copy-start(bf16[360,768]{1,0:T(8,128)(2,1)S(1)} %reshape.661) | copy-start | bytes 1658884
  124.7 2.7 copy-start.16
  124.7 2.7 copy-start.24
  137.3 357.9 %all-reduce.16.cloned.1.call-start = ((), (), s32[]{:S(2)}) async-start(), calls=%async_computation.9 | async-start | bytes 3145728 | tf_op jit(solution)/shard_map/psum | solution.py:184
  186.3 3.5 copy-start.9
  189.8 1.2 copy-start.20
  189.8 1.3 copy-start.25
  193.5 1.4 copy-start.15
  196.6 2.0 copy-start.4
  198.5 2.5 copy-start.10
  198.5 1.2 copy-start.2
  205.7 365.9 %reduce-scatter.7.cloned.1.call-start = ((), (), s32[]{:S(2)}) async-start(), calls=%async_computation.8 | async-start | bytes 9584640
  364.7 1.9 copy-start.6
  364.7 1.9 copy-start.11
  370.6 1.9 copy-start.7
  373.3 3.0 copy-start.12
  379.7 118.1 %all-to-all-start.4 = ((f32[4,64,1,768]{3,0,2,1:T(4,128)}), f32[4,64,1,768]{3,0,2,1:T(4,128)S(1)}, u32[]{:S(2)}, u32[]{:S(2)}) async-start(f32[4,64,1,768]{3,0,2,1:T(4,128)} %copy.86), calls=%async_computation.4 | async-start | bytes 1572864 | tf_op jit(solution)/shard_map/all_to_all | solution.py:15
  (6 other events, 5.0 us)
Sparse Core Ops, SparseCore 0:
  137.4 217.5 reduce-scatter.4
  364.8 173.4 reduce-scatter.6
Sparse Core Ops, SparseCore 1:
  205.8 289.3 all-reduce.15
where the time goes:
time: 591 us; the launch traced here: 582 us
  waiting for transfers between devices  290 us (49%)
  blocking collectives  94.9 us (16%)
  matrix products  80.1 us (14%)
  local copies, waits for them, and re-layouts  42 us (7%)
  starting transfers between devices  34.8 us (6%)
  other arithmetic  24.1 us (4%)
  between operations  16.9 us (3%)
    reduce_scatter x1, waiting for transfers between devices, side_by_side(): result = lax.psum_scatter(both, axis, scatter_dimension=dim, tiled=True)  149 us
    psum x1, waiting for transfers between devices, local(): lax.psum((grad_gain_one, grad_gain_two, pulled[2], pulled[3], pulled[4],...  101 us
    psum x1, blocking collectives, local(): lax.psum((grad_gain_one, grad_gain_two, pulled[2], pulled[3], pulled[4],...  64.9 us
    all_to_all x1, blocking collectives, in_one_piece(): lax.all_to_all(both, axis, split_axis=split_dim, concat_axis=concat_dim,...  30.1 us
    all_to_all x3, waiting for transfers between devices, in_one_piece(): lax.all_to_all(both, axis, split_axis=split_dim, concat_axis=concat_dim,...  27 us
    all_to_all x3, starting transfers between devices, in_one_piece(): lax.all_to_all(both, axis, split_axis=split_dim, concat_axis=concat_dim,...  21.8 us
    unnamed x69, local copies, waits for them, and re-layouts  17 us
    dot_general x16, matrix products, meridian_apply(): return jnp.einsum('hk,bhmd->bkmd', table, field, precision=highest)  13.3 us
  transfers between devices with their start and end apart: 7, of which 5 were waited for; matrix products, arithmetic and copies ran while one was open for 14% of the time, Pallas kernels for 0%

commit v1 on v0

--- a/solution.py
+++ b/solution.py
@@ -182,17 +182,20 @@
     bias_sum = jnp.sum(grad_hidden, axis=0)
     out_sum = jnp.sum(cotangent, axis=(0, 1, 2), dtype=jnp.float32)
     totals = lax.psum(
-        (
-            grad_gain_one,
-            grad_gain_two,
-            pulled[2],
-            pulled[3],
-            pulled[4],
-            pulled[5],
-            bias_sum,
-            out_sum,
+        lax.psum(
+            (
+                grad_gain_one,
+                grad_gain_two,
+                pulled[2],
+                pulled[3],
+                pulled[4],
+                pulled[5],
+                bias_sum,
+                out_sum,
+            ),
+            "space",
         ),
-        ("dp", "space"),
+        "dp",
     )
     paired = side_by_side((term_one, term_two), "dp", 1, 0)
     summed = side_by_side((paired[0], paired[1]), "space", 1, 0)

time: 591 us -> 1420 us (2.40)
  waiting for transfers between devices: 290 us -> 855 us
  blocking collectives: 94.9 us -> 323 us
  matrix products: 80.1 us -> 94.5 us
    psum x1, waiting for transfers between devices: 101 us -> 797 us  [local(): lax.psum((grad_gain_one, grad_gain_two, pulled[2], pulled[3], pulled[4],...]
    psum x1, blocking collectives: 64.9 us -> 317 us  [local(): lax.psum((grad_gain_one, grad_gain_two, pulled[2], pulled[3], pulled[4],...]
    reduce_scatter x1, waiting for transfers between devices: 149 us -> 0.03 us  [side_by_side(): result = lax.psum_scatter(both, axis, scatter_dimension=dim, tiled=True)]
    all_to_all x1 -> x0, blocking collectives: 30.1 us -> none  [in_one_piece(): lax.all_to_all(both, axis, split_axis=split_dim, concat_axis=concat_dim,...]
    all_to_all x3 -> x4, waiting for transfers between devices: 27 us -> 46.5 us  [in_one_piece(): lax.all_to_all(both, axis, split_axis=split_dim, concat_axis=concat_dim,...]
  transfers between devices with their start and end apart: 7 -> 9, of which waited for: 5 -> 5; matrix products, arithmetic and copies ran while one was open for 14% -> 6% of each run, Pallas kernels for 0% -> 0%
where the time goes in v1:
time: 1420 us; the launch traced here: 1400 us
  waiting for transfers between devices  855 us (60%)
  blocking collectives  323 us (23%)
  matrix products  94.5 us (7%)
  local copies, waits for them, and re-layouts  43.6 us (3%)
  starting transfers between devices  37.5 us (3%)
  other arithmetic  32.6 us (2%)
  between operations  16.6 us (1%)
    psum x1, waiting for transfers between devices, local(): lax.psum((grad_gain_one, grad_gain_two, pulled[2], pulled[3], pulled[4],...  797 us
    psum x1, blocking collectives, local(): lax.psum((grad_gain_one, grad_gain_two, pulled[2], pulled[3], pulled[4],...  317 us
    all_to_all x4, waiting for transfers between devices, in_one_piece(): lax.all_to_all(both, axis, split_axis=split_dim, concat_axis=concat_dim,...  46.5 us
  transfers between devices with their start and end apart: 9, of which 5 were waited for; matrix products, arithmetic and copies ran while one was open for 6% of the time, Pallas kernels for 0%

profile of v1, /device:TPU:1, one launch (start us, length us, event | category | flops | bytes accessed | tf_op | source)
XLA Modules:
  0.0 1402.6 jit_solution(7764050215067676864)
XLA Ops:
  8.0 12.5 all-to-all-start
  20.5 2.7 sort.17
  23.2 11.9 all-to-all-done
  35.1 1.7 gather_fusion
  44.4 4.9 all-to-all-start.1
  49.6 16.6 %all-to-all-done.1 = f32[4,1,64,768]{3,0,1,2:T(4,128)S(1)} async-done(((f32[4,1,64,768]{3,0,1,2:T(4,128)}), f32[4,1,64,768]{3,0,1,2:T(4,128)S(1)}, u32[]{:S(2)}, u32[]{:S(2)}) %all-to-all-start.1) | async-done | bytes 786464 | tf_op jit(solution)/shard_map/all_to_all | solution.py:15
  80.9 1.8 fusion.19
  87.0 4.7 all-to-all-start.2
  91.9 6.5 fusion.414
  98.4 10.4 all-to-all-done.2
  113.5 9.5 fusion.404
  124.4 5.2 fusion.34
  138.4 4.5 all-to-all-start.3
  143.2 8.2 fusion.32
  151.4 8.7 convolution_bitcast_fusion
  165.1 2.9 convolution_bitcast_fusion.7
  168.1 1.9 convolution_bitcast_fusion.8
  171.4 2.0 reshape.679
  173.4 2.4 convolution_bitcast_fusion.5
  178.9 1.9 fusion.70
  188.3 14.4 %pad_maximum_fusion = f32[1536,3072]{1,0:T(8,128)} fusion(f32[768,3072]{1,0:T(8,128)} %convolution_bitcast_fusion, f32[768,3072]{1,0:T(8,128)} %fusion.32), kind=kLoop, calls=%fused_computation.1 | loop fusion | flops 4718592 | bytes 37748736 | tf_op jit(solution)/shard_map/concatenate | solution.py:27
  202.8 796.7 %all-reduce.19.cloned.1.call-done = (f32[2,8,96,96]{3,2,1,0:T(8,128)}, f32[2,8,96,96]{3,2,1,0:T(8,128)}) async-done(((f32[2,8,96,96]{3,2,1,0:T(8,128)}, f32[2,8,96,96]{3,2,1,0:T(8,128)}), (f32[2,8,96,96]{3,2,1,0:T(8,128)}, f32[2,8,96,96]{3,2,1,0:T(8,128)})) %all-reduce.19.cloned.1.call-update) | async-done | bytes 1179664 | tf_op jit(solution)/shard_map/psum | solution.py:185
  1000.0 9.7 copy.108
  1009.7 1.9 fusion.140
  1013.6 2.0 reshape.686
  1015.6 1.9 fusion.146
  1024.7 10.2 all-to-all-start.4
  1036.8 19.5 %all-to-all-done.4 = f32[4,64,1,768]{3,0,2,1:T(4,128)S(1)} async-done(((f32[4,64,1,768]{3,0,2,1:T(4,128)}), f32[4,64,1,768]{3,0,2,1:T(4,128)S(1)}, u32[]{:S(2)}, u32[]{:S(2)}) %all-to-all-start.4) | async-done | bytes 786464 | tf_op jit(solution)/shard_map/all_to_all | solution.py:15
  1060.6 2.1 copy.93
  1062.8 317.0 %all-reduce.12 = (f32[3072]{0:T(1024)S(1)}, f32[768]{0:T(1024)S(1)}, f32[768]{0:T(1024)S(1)}, f32[768]{0:T(1024)S(1)}, f32[2,768]{1,0:T(2,128)S(1)}, /*index=5*/f32[2,768]{1,0:T(2,128)S(1)}) all-reduce(f32[3072]{0:T(1024)S(1)} %get-tuple-element.70, f32[768]{0:T(1024)S(1)} %get-tuple-element.80, ...), channel_id=1, replica_groups=mesh['dp'=2,'space'=64] {'space'}, use_global_device_ids=true, to_apply=%region_12.13 | all-reduce | flops 8448 | bytes 67584 | tf_op jit(solution)/shard_map/psum | solution.py:185
  1379.8 5.6 all-reduce.14
  1388.9 2.2 broadcast_multiply_fusion.1
  (209 shorter events, 81.9 us)
Async XLA Ops:
  8.0 27.1 %all-to-all-start = ((bf16[1,64,2,2160]{3,2,0,1:T(2,128)(2,1)}), bf16[1,64,2,2160]{3,2,0,1:T(2,128)(2,1)S(1)}, u32[]{:S(2)}, u32[]{:S(2)}) async-start(bf16[1,64,2,2160]{3,2,0,1:T(2,128)(2,1)} %bitcast.618), calls=%async_computation | async-start | bytes 1114112 | tf_op jit(solution)/shard_map/all_to_all | solution.py:122
  44.4 4.9 copy-start.35
  44.4 5.1 copy-start.36
  44.4 21.8 %all-to-all-start.1 = ((f32[4,1,64,768]{3,0,1,2:T(4,128)}), f32[4,1,64,768]{3,0,1,2:T(4,128)S(1)}, u32[]{:S(2)}, u32[]{:S(2)}) async-start(f32[4,1,64,768]{3,0,1,2:T(4,128)} %copy.66), calls=%async_computation.1 | async-start | bytes 1572864 | tf_op jit(solution)/shard_map/all_to_all | solution.py:15
  69.7 2.1 copy-start.1
  69.7 2.1 copy-start.26
  74.5 3.7 copy-start.3
  75.8 2.4 copy-start.22
  78.9 2.0 copy-start.8
  87.0 4.7 copy-start.19
  87.0 21.8 %all-to-all-start.2 = ((f32[4,64,1,768]{3,0,2,1:T(4,128)}), f32[4,64,1,768]{3,0,2,1:T(4,128)S(1)}, u32[]{:S(2)}, u32[]{:S(2)}) async-start(f32[4,64,1,768]{3,0,2,1:T(4,128)} %copy.75), calls=%async_computation.2 | async-start | bytes 1572864 | tf_op jit(solution)/shard_map/all_to_all | solution.py:15
  91.9 6.5 copy-start.28
  113.5 9.5 copy-start.21
  138.4 21.7 %all-to-all-start.3 = ((f32[4,1,64,768]{3,0,1,2:T(4,128)}), f32[4,1,64,768]{3,0,1,2:T(4,128)S(1)}, u32[]{:S(2)}, u32[]{:S(2)}) async-start(f32[4,1,64,768]{3,0,1,2:T(4,128)} %copy.78), calls=%async_computation.3 | async-start | bytes 1572864 | tf_op jit(solution)/shard_map/all_to_all | solution.py:15
  143.0 856.5 %all-reduce.19.cloned.1.call-start = ((), (), s32[]{:S(2)}) async-start(), calls=%async_computation.9 | async-start | bytes 3145728 | tf_op jit(solution)/shard_map/psum | solution.py:185
  143.2 8.3 copy-start.29
  160.4 3.4 copy-start.13
  163.8 4.2 copy-start.9
  168.1 1.9 copy-start.25
  173.4 2.4 copy-start.30
  178.9 1.9 copy-start.4
  180.8 2.3 copy-start.10
  184.7 2.1 copy-start.31
  184.7 2.1 copy-start.32
  188.2 811.7 %reduce-scatter.5.cloned.1.call-start = ((), (), s32[]{:S(2)}) async-start(), calls=%async_computation.7 | async-start | bytes 28311552 | tf_op jit(solution)/shard_map/reduce_scatter | solution.py:28
  202.7 1186.2 %all-reduce.21.cloned.1.call-start = ((), (), s32[]{:S(2)}) async-start(), calls=%async_computation.10 | async-start | bytes 3145728 | tf_op jit(solution)/shard_map/psum | solution.py:184
  999.5 392.6 %reduce-scatter.7.cloned.1.call-start = ((), (), s32[]{:S(2)}) async-start(), calls=%async_computation.8 | async-start | bytes 9584640
  1009.7 1.9 copy-start.6
  1009.7 1.9 copy-start.11
  1018.3 3.0 copy-start.12
  1024.7 31.5 %all-to-all-start.4 = ((f32[4,64,1,768]{3,0,2,1:T(4,128)}), f32[4,64,1,768]{3,0,2,1:T(4,128)S(1)}, u32[]{:S(2)}, u32[]{:S(2)}) async-start(f32[4,64,1,768]{3,0,2,1:T(4,128)} %copy.86), calls=%async_computation.4 | async-start | bytes 1572864 | tf_op jit(solution)/shard_map/all_to_all | solution.py:15
  1388.9 2.2 copy-start.27
  (15 other events, 18.6 us)
Sparse Core Ops, SparseCore 0:
  188.4 811.0 all-reduce.18
  1009.8 170.9 reduce-scatter.6
Sparse Core Ops, SparseCore 1:
  202.8 217.0 reduce-scatter.4
  999.6 61.8 all-reduce.20
